TPU v7x, 32 devices: a whole 2x2x4 slice. The times are simulated.
32 devices in a mesh: lon: 8 (over z, y), lat: 4 (over x, core).
Axes of the slice: x: 2, y: 2, z: 4, core: 2. Of those that a mesh axis runs over, the one named last changes fastest.
Arguments:
- ocean_state: float32 [4, 8, 64, 1024], P(None, None, 'lat', 'lon'), may hold values from -5 to 5
- thickness: float32 [8, 64, 1024], P(None, 'lat', 'lon'), may hold values from 0.5 to 2
- wet_mask: int32 [8, 64, 1024], P(None, 'lat', 'lon'), may hold values 0 or 1
- mode_counts: int32 [64], P('lat'), may hold values from 1 to 64, as said below
- row_flags: int32 [64], P('lat'), may hold values from 0 to 1, as said below
Outputs:
- ocean_next: float32 [4, 8, 64, 1024], P(None, None, 'lat', 'lon')
Inputs may be any that keep to these rules, and one draw needn't show every extreme that they name: `mode_counts`: mode counts lie in the range; row 0 keeps 64. `row_flags`: only rows among the first 16 or the last 16 are flagged; the first and the last row always are.
All inputs are finite; a program needn't handle non-finite values. No bound on the sum of `wet_mask` on one device may be relied on, other than what follows from the above.
Results may differ from a plain program's by a relative error of at most 0.0003.
Values sent between devices are 32-bit elements; how exact they have to be, the bound alone decides.
No kernel may reach another device: no remote copies, remote signals or barrier semaphores. Data moves between devices by JAX's collectives and lax.ppermute only.
A program may use at most 64 MiB of HBM per device.

v0:
```python
import math
import jax
import jax.numpy as jnp
from jax import lax
from jax.sharding import PartitionSpec as P

FBAND = 16
MAXM = 64
lat_edge = 1.3
diffusion = 0.05
vertical_mix = 0.5
time_step = 0.05


def with_halo(array, sides, width, wrap):
    for axis, dim in sides:
        peers, length = (lax.axis_size(axis), array.shape[dim])
        up = [(i, (i + 1) % peers) for i in range(peers if wrap else peers - 1)]
        down = [(j, i) for i, j in up]
        last = lax.slice_in_dim(array, length - width, length, axis=dim)
        leading = lax.slice_in_dim(array, 0, width, axis=dim)
        before = lax.ppermute(last, axis, up)
        after = lax.ppermute(leading, axis, down)
        array = jnp.concatenate([before, array, after], axis=dim)
    return array


def advance(padded, u_pad, v_pad, static, centre, faces):
    thick = static[0]
    wet = static[1]
    inv_c = 1.0 / centre
    east_u = 0.5 * (u_pad[:, :, :-1] + u_pad[:, :, 1:])
    east_h = 0.5 * (thick[:, :, :-1] + thick[:, :, 1:]) * wet[:, :, :-1] * wet[:, :, 1:]
    flux_e = east_h[None] * (
        east_u[None] * 0.5 * (padded[..., :-1] + padded[..., 1:])
        - diffusion * (padded[..., 1:] - padded[..., :-1]) * inv_c[:, None]
    )
    zonal = (flux_e[..., 1:] - flux_e[..., :-1])[:, :, 1:-1, :] * inv_c[1:-1, None]
    north_v = 0.5 * (v_pad[:, :-1, :] + v_pad[:, 1:, :])
    north_h = (
        0.5 * (thick[:, :-1, :] + thick[:, 1:, :]) * wet[:, :-1, :] * wet[:, 1:, :] * faces[:, None]
    )
    flux_n = north_h[None] * (
        north_v[None] * 0.5 * (padded[:, :, :-1] + padded[:, :, 1:])
        - diffusion * (padded[:, :, 1:] - padded[:, :, :-1])
    )
    merid = (flux_n[:, :, 1:] - flux_n[:, :, :-1])[..., 1:-1] * inv_c[1:-1, None]
    inner = padded[:, :, 1:-1, 1:-1]
    wet_in = wet[:, 1:-1, 1:-1]
    thick_in = jnp.where(wet_in > 0, thick[:, 1:-1, 1:-1], 1.0)
    coupling = wet_in[:-1] * wet_in[1:] * vertical_mix / (0.5 * (thick_in[:-1] + thick_in[1:]))
    vmix = coupling[None] * (inner[:, 1:] - inner[:, :-1])
    empty = jnp.zeros_like(vmix[:, :1])
    vert = jnp.concatenate([vmix, empty], axis=1) - jnp.concatenate([empty, vmix], axis=1)
    return inner + wet_in[None] * time_step * (vert - zonal - merid) / thick_in[None]


def mode_basis(index, length, modes):
    turns = jnp.arange(modes, dtype=jnp.int32)[None, :] * index[:, None] % length
    angle = turns.astype(jnp.float32) * (2.0 * math.pi / length)
    return jnp.concatenate([jnp.cos(angle), jnp.sin(angle)], axis=1)


def mode_weights(counts, modes, length):
    order = jnp.arange(modes).astype(jnp.float32)
    keep = (order[None, :] < counts[:, None]).astype(jnp.float32)
    scale = jnp.where(order == 0, 1.0, 2.0) / length
    weights = keep * scale[None, :]
    return jnp.concatenate([weights, weights], axis=1)


def extend(fields, width):
    wider = with_halo(fields, (("lon", 3),), width, True)
    return with_halo(wider, (("lat", 2),), width, False)


def shards(ocean_state, thickness, wet_mask, mode_counts, row_flags):
    wet = wet_mask.astype(jnp.float32)
    static = jnp.stack([thickness, wet])
    levels = ocean_state.shape[1]
    rows = ocean_state.shape[2]
    lanes = ocean_state.shape[3]
    nlat = rows * lax.axis_size("lat")
    nlon = lanes * lax.axis_size("lon")
    lat_pos = lax.axis_index("lat")
    lon_pos = lax.axis_index("lon")
    joined = extend(jnp.concatenate([ocean_state, static], axis=0), 1)
    fields = joined[:4]
    fixed = joined[4:]
    index = lat_pos * rows - 1 + jnp.arange(rows + 2 * 1, dtype=jnp.int32)
    place = index.astype(jnp.float32)
    centre = jnp.cos(lat_edge * (2.0 * (place + 0.5) / nlat - 1.0))
    faces = jnp.cos(lat_edge * (2.0 * (place[:-1] + 1.0) / nlat - 1.0))
    centre, faces = (centre, faces)
    state = advance(fields, fields[2], fields[3], fixed, centre, faces)
    fields = extend(state, 1)
    state = advance(fields, fields[2], fields[3], fixed, centre, faces)
    flags = row_flags.astype(jnp.float32)
    counts = mode_counts.astype(jnp.float32)
    total = 4 * levels * FBAND
    flat = state.reshape(total, lanes)
    row_counts = jnp.broadcast_to(counts[None, None, :], (4, levels, FBAND)).reshape(total)
    index = lon_pos * lanes + jnp.arange(lanes, dtype=jnp.int32)
    basis = mode_basis(index, nlon, MAXM)
    partial_sum = jnp.dot(
        flat, basis, precision=lax.Precision.HIGHEST, preferred_element_type=jnp.float32
    )
    totals = lax.psum(partial_sum, "lon")
    smooth = jnp.dot(
        totals * mode_weights(row_counts, MAXM, nlon),
        basis.T,
        precision=lax.Precision.HIGHEST,
        preferred_element_type=jnp.float32,
    )
    smooth = smooth.reshape(4, levels, FBAND, lanes)
    filtered = state + flags[None, None, :, None] * wet[None] * (smooth - state)
    return filtered


def solution(mesh):
    in_specs = (
        P(None, None, "lat", "lon"),
        P(None, "lat", "lon"),
        P(None, "lat", "lon"),
        P("lat"),
        P("lat"),
    )
    out_specs = P(None, None, "lat", "lon")
    return jax.shard_map(shards, mesh=mesh, in_specs=in_specs, out_specs=out_specs, check_vma=False)
```

profile of v0, /device:TPU:0, one launch (start us, length us, event | category | flops | bytes accessed | tf_op | source)
XLA Modules:
  0.0 145.7 jit_solution(13678122371583939406)
XLA Ops:
  6.5 0.8 convert_bitcast_fusion
  7.4 1.1 pad_maximum_fusion.13
  8.5 0.2 fusion.44
  8.7 6.1 %collective-permute-start.1 = (f32[6,8,16,1]{3,2,1,0:T(8,128)S(1)}, f32[6,8,16,1]{3,2,1,0:T(8,128)S(1)}, u32[]{:S(2)}, u32[]{:S(2)}) collective-permute-start(f32[6,8,16,1]{3,2,1,0:T(8,128)S(1)} %get-tuple-element.24), channel_id=1, source_target_pairs={{4,0},{8,4},{12,8},{16,12},{20,16},{24,20},{28,24},{0,28},{5,1},{9... | collective-permute-start | bytes 9224 | tf_op jit(solution)/shard_map/ppermute | solution.py:23
  14.8 0.3 fusion.35
  15.3 13.9 %collective-permute-done.1 = f32[6,8,16,1]{3,2,1,0:T(8,128)S(1)} collective-permute-done((f32[6,8,16,1]{3,2,1,0:T(8,128)S(1)}, f32[6,8,16,1]{3,2,1,0:T(8,128)S(1)}, u32[]{:S(2)}, u32[]{:S(2)}) %collective-permute-start.1) | collective-permute-done | bytes 3104 | tf_op jit(solution)/shard_map/ppermute | solution.py:23
  29.4 0.4 pad_maximum_fusion.15
  29.8 1.9 %collective-permute-start.2 = (f32[6,8,1,130]{3,2,1,0:T(1,128)S(1)}, f32[6,8,1,130]{3,2,1,0:T(1,128)S(1)}, u32[]{:S(2)}, u32[]{:S(2)}) collective-permute-start(f32[6,8,1,130]{3,2,1,0:T(1,128)S(1)} %get-tuple-element.10), channel_id=1, source_target_pairs={{0,1},{1,2},{2,3},{4,5},{5,6},{6,7},{8,9},{9,10},{10,11},{12,13},{... | collective-permute-start | bytes 74888 | tf_op jit(solution)/shard_map/ppermute | solution.py:22
  31.7 1.3 collective-permute-start.3
  33.1 2.9 %collective-permute-done.3 = f32[6,8,1,130]{3,2,1,0:T(1,128)S(1)} collective-permute-done((f32[6,8,1,130]{3,2,1,0:T(1,128)S(1)}, f32[6,8,1,130]{3,2,1,0:T(1,128)S(1)}, u32[]{:S(2)}, u32[]{:S(2)}) %collective-permute-start.3) | collective-permute-done | bytes 24992 | tf_op jit(solution)/shard_map/ppermute | solution.py:23
  36.0 0.5 pad_maximum_fusion
  36.8 0.6 subtract_multiply_fusion.2
  37.5 0.2 fusion.23
  37.8 0.3 subtract_multiply_fusion.3
  38.0 0.2 fusion.42
  38.4 0.3 fusion.11
  38.8 4.8 %collective-permute-start.5 = (f32[4,8,16,1]{3,2,1,0:T(8,128)S(1)}, f32[4,8,16,1]{3,2,1,0:T(8,128)S(1)}, u32[]{:S(2)}, u32[]{:S(2)}) collective-permute-start(f32[4,8,16,1]{3,2,1,0:T(8,128)S(1)} %get-tuple-element.26), channel_id=1, source_target_pairs={{4,0},{8,4},{12,8},{16,12},{20,16},{24,20},{28,24},{0,28},{5,1},{9... | collective-permute-start | bytes 6152 | tf_op jit(solution)/shard_map/ppermute | solution.py:23
  43.6 4.8 %collective-permute-done.5 = f32[4,8,16,1]{3,2,1,0:T(8,128)S(1)} collective-permute-done((f32[4,8,16,1]{3,2,1,0:T(8,128)S(1)}, f32[4,8,16,1]{3,2,1,0:T(8,128)S(1)}, u32[]{:S(2)}, u32[]{:S(2)}) %collective-permute-start.5) | collective-permute-done | bytes 2080 | tf_op jit(solution)/shard_map/ppermute | solution.py:23
  48.4 5.9 %collective-permute-done.4 = f32[4,8,16,1]{3,2,1,0:T(8,128)S(1)} collective-permute-done((f32[4,8,16,1]{3,2,1,0:T(8,128)S(1)}, f32[4,8,16,1]{3,2,1,0:T(8,128)S(1)}, u32[]{:S(2)}, u32[]{:S(2)}) %collective-permute-start.4) | collective-permute-done | bytes 2080 | tf_op jit(solution)/shard_map/ppermute | solution.py:22
  54.3 0.3 pad_maximum_fusion.22
  54.6 1.3 collective-permute-start.7
  55.9 3.5 %collective-permute-start.6 = (f32[4,8,1,130]{3,2,1,0:T(1,128)S(1)}, f32[4,8,1,130]{3,2,1,0:T(1,128)S(1)}, u32[]{:S(2)}, u32[]{:S(2)}) collective-permute-start(f32[4,8,1,130]{3,2,1,0:T(1,128)S(1)} %get-tuple-element.17), channel_id=1, source_target_pairs={{0,1},{1,2},{2,3},{4,5},{5,6},{6,7},{8,9},{9,10},{10,11},{12,13},{... | collective-permute-start | bytes 49928 | tf_op jit(solution)/shard_map/ppermute | solution.py:22
  59.5 0.8 collective-permute-done.6
  60.2 0.4 pad_maximum_fusion.11
  60.7 0.6 subtract_multiply_fusion
  61.6 0.3 subtract_multiply_fusion.1
  61.9 0.2 fusion.40
  62.0 0.3 fusion.4
  62.3 1.1 fusion.36
  63.7 73.0 %all-reduce.6.cloned.1.call-done = f32[512,128]{1,0:T(8,128)} async-done(((f32[512,128]{1,0:T(8,128)}), f32[512,128]{1,0:T(8,128)}) %all-reduce.6.cloned.1.call-update) | async-done | bytes 262160 | tf_op jit(solution)/shard_map/psum | solution.py:108
  136.7 1.4 fusion.14
  138.1 0.7 multiply_add_fusion
  (43 shorter events, 1.7 us)
Async XLA Ops:
  6.5 130.2 %all-reduce.6.cloned.1.call-start = ((), (), s32[]{:S(2)}) async-start(), calls=%async_computation | async-start | bytes 524288 | tf_op jit(solution)/shard_map/psum | solution.py:108
  7.4 7.7 %copy-start.3 = (s32[16]{0:T(128)S(1)}, s32[16]{0:T(128)}, u32[]{:S(2)}) copy-start(s32[16]{0:T(128)} %param.9) | copy-start | bytes 196
  7.4 7.8 %copy-start.2 = (s32[8,16,128]{2,1,0:T(8,128)S(1)}, s32[8,16,128]{2,1,0:T(8,128)}, u32[]{:S(2)}) copy-start(s32[8,16,128]{2,1,0:T(8,128)} %param.7) | copy-start | bytes 196612
  7.4 22.0 %copy-start = (f32[4,8,16,128]{3,2,1,0:T(8,128)S(1)}, f32[4,8,16,128]{3,2,1,0:T(8,128)}, u32[]{:S(2)}) copy-start(f32[4,8,16,128]{3,2,1,0:T(8,128)} %param.5) | copy-start | bytes 786436
  7.4 22.0 %copy-start.1 = (f32[8,16,128]{2,1,0:T(8,128)S(1)}, f32[8,16,128]{2,1,0:T(8,128)}, u32[]{:S(2)}) copy-start(f32[8,16,128]{2,1,0:T(8,128)} %param.6) | copy-start | bytes 196612
  8.7 20.6 %collective-permute-start.1 = (f32[6,8,16,1]{3,2,1,0:T(8,128)S(1)}, f32[6,8,16,1]{3,2,1,0:T(8,128)S(1)}, u32[]{:S(2)}, u32[]{:S(2)}) collective-permute-start(f32[6,8,16,1]{3,2,1,0:T(8,128)S(1)} %get-tuple-element.24), channel_id=1, source_target_pairs={{4,0},{8,4},{12,8},{16,12},{20,16},{24,20},{28,24},{0,28},{5,1},{9... | collective-permute-start | bytes 9224 | tf_op jit(solution)/shard_map/ppermute | solution.py:23
  14.7 14.7 %collective-permute-start = (f32[6,8,16,1]{3,2,1,0:T(8,128)S(1)}, f32[6,8,16,1]{3,2,1,0:T(8,128)S(1)}, u32[]{:S(2)}, u32[]{:S(2)}) collective-permute-start(f32[6,8,16,1]{3,2,1,0:T(8,128)S(1)} %get-tuple-element.23), channel_id=1, source_target_pairs={{0,4},{4,8},{8,12},{12,16},{16,20},{20,24},{24,28},{28,0},{1,5},{5... | collective-permute-start | bytes 9224 | tf_op jit(solution)/shard_map/ppermute | solution.py:22
  29.8 3.4 %collective-permute-start.2 = (f32[6,8,1,130]{3,2,1,0:T(1,128)S(1)}, f32[6,8,1,130]{3,2,1,0:T(1,128)S(1)}, u32[]{:S(2)}, u32[]{:S(2)}) collective-permute-start(f32[6,8,1,130]{3,2,1,0:T(1,128)S(1)} %get-tuple-element.10), channel_id=1, source_target_pairs={{0,1},{1,2},{2,3},{4,5},{5,6},{6,7},{8,9},{9,10},{10,11},{12,13},{... | collective-permute-start | bytes 74888 | tf_op jit(solution)/shard_map/ppermute | solution.py:22
  31.7 4.3 %collective-permute-start.3 = (f32[6,8,1,130]{3,2,1,0:T(1,128)S(1)}, f32[6,8,1,130]{3,2,1,0:T(1,128)S(1)}, u32[]{:S(2)}, u32[]{:S(2)}) collective-permute-start(f32[6,8,1,130]{3,2,1,0:T(1,128)S(1)} %get-tuple-element.9), channel_id=1, source_target_pairs={{1,0},{2,1},{3,2},{5,4},{6,5},{7,6},{9,8},{10,9},{11,10},{13,12},{... | collective-permute-start | bytes 74888 | tf_op jit(solution)/shard_map/ppermute | solution.py:23
  38.8 9.6 %collective-permute-start.5 = (f32[4,8,16,1]{3,2,1,0:T(8,128)S(1)}, f32[4,8,16,1]{3,2,1,0:T(8,128)S(1)}, u32[]{:S(2)}, u32[]{:S(2)}) collective-permute-start(f32[4,8,16,1]{3,2,1,0:T(8,128)S(1)} %get-tuple-element.26), channel_id=1, source_target_pairs={{4,0},{8,4},{12,8},{16,12},{20,16},{24,20},{28,24},{0,28},{5,1},{9... | collective-permute-start | bytes 6152 | tf_op jit(solution)/shard_map/ppermute | solution.py:23
  43.6 10.8 %collective-permute-start.4 = (f32[4,8,16,1]{3,2,1,0:T(8,128)S(1)}, f32[4,8,16,1]{3,2,1,0:T(8,128)S(1)}, u32[]{:S(2)}, u32[]{:S(2)}) collective-permute-start(f32[4,8,16,1]{3,2,1,0:T(8,128)S(1)} %get-tuple-element.25), channel_id=1, source_target_pairs={{0,4},{4,8},{8,12},{12,16},{16,20},{20,24},{24,28},{28,0},{1,5},{5... | collective-permute-start | bytes 6152 | tf_op jit(solution)/shard_map/ppermute | solution.py:22
  54.6 4.8 %collective-permute-start.7 = (f32[4,8,1,130]{3,2,1,0:T(1,128)S(1)}, f32[4,8,1,130]{3,2,1,0:T(1,128)S(1)}, u32[]{:S(2)}, u32[]{:S(2)}) collective-permute-start(f32[4,8,1,130]{3,2,1,0:T(1,128)S(1)} %get-tuple-element.18), channel_id=1, source_target_pairs={{1,0},{2,1},{3,2},{5,4},{6,5},{7,6},{9,8},{10,9},{11,10},{13,12},{... | collective-permute-start | bytes 49928 | tf_op jit(solution)/shard_map/ppermute | solution.py:23
  55.9 4.3 %collective-permute-start.6 = (f32[4,8,1,130]{3,2,1,0:T(1,128)S(1)}, f32[4,8,1,130]{3,2,1,0:T(1,128)S(1)}, u32[]{:S(2)}, u32[]{:S(2)}) collective-permute-start(f32[4,8,1,130]{3,2,1,0:T(1,128)S(1)} %get-tuple-element.17), channel_id=1, source_target_pairs={{0,1},{1,2},{2,3},{4,5},{5,6},{6,7},{8,9},{9,10},{10,11},{12,13},{... | collective-permute-start | bytes 49928 | tf_op jit(solution)/shard_map/ppermute | solution.py:22
  62.0 1.5 copy-start.4
Sparse Core Ops, SparseCore 0:
  63.6 73.0 all-reduce.5
where the time goes:
time: 146 us
  waiting for transfers between devices  101 us (69%)
  starting transfers between devices  18.9 us (13%)
  between operations  13.7 us (9%)
  other arithmetic  7.99 us (5%)
  matrix products  2.53 us (2%)
    psum x1, waiting for transfers between devices, shards(): totals = lax.psum(partial_sum, 'lon')  73 us
    ppermute x4, waiting for transfers between devices, with_halo(): after = lax.ppermute(leading, axis, down)  21.6 us
    ppermute x4, starting transfers between devices, with_halo(): after = lax.ppermute(leading, axis, down)  13.5 us
    ppermute x4, waiting for transfers between devices, with_halo(): before = lax.ppermute(last, axis, up)  6.89 us
    ppermute x4, starting transfers between devices, with_halo(): before = lax.ppermute(last, axis, up)  5.41 us
  transfers between devices with their start and end apart: 9, of which 7 were waited for; matrix products, arithmetic and copies ran while one was open for 1% of the time, Pallas kernels for 0%

commit v1 on v0

--- a/solution.py
+++ b/solution.py
@@ -105,7 +105,9 @@
     partial_sum = jnp.dot(
         flat, basis, precision=lax.Precision.HIGHEST, preferred_element_type=jnp.float32
     )
-    totals = lax.psum(partial_sum, "lon")
+    totals = partial_sum
+    for hop in (1, 2, 4):
+        totals = totals + lax.ppermute(totals, "lon", [(dev, dev ^ hop) for dev in range(8)])
     smooth = jnp.dot(
         totals * mode_weights(row_counts, MAXM, nlon),
         basis.T,

time: 146 us -> 89.7 us (0.61)
  waiting for transfers between devices: 101 us -> 57.4 us
  between operations: 13.7 us -> 0.3 us
  starting transfers between devices: 18.9 us -> 21.7 us
  matrix products: 2.53 us -> 0.9 us
    psum x1 -> x0, waiting for transfers between devices: 73 us -> none  [shards(): totals = lax.psum(partial_sum, 'lon')]
    ppermute x0 -> x3, waiting for transfers between devices: none -> 28.8 us  [shards(): lax.ppermute(totals, 'lon', [(dev, dev ^ hop) for dev in range(8)])]
    ppermute x0 -> x3, starting transfers between devices: none -> 2.81 us  [shards(): lax.ppermute(totals, 'lon', [(dev, dev ^ hop) for dev in range(8)])]
  transfers between devices with their start and end apart: 9 -> 11, of which waited for: 7 -> 9; matrix products, arithmetic and copies ran while one was open for 1% -> 1% of each run, Pallas kernels for 0% -> 0%
where the time goes in v1:
time: 89.7 us; the launch traced here: 89.4 us
  waiting for transfers between devices  57.4 us (64%)
  starting transfers between devices  21.7 us (24%)
  other arithmetic  8.05 us (9%)
  local copies, waits for them, and re-layouts  1.09 us (1%)
  matrix products  0.9 us (1%)
    ppermute x3, waiting for transfers between devices, shards(): lax.ppermute(totals, 'lon', [(dev, dev ^ hop) for dev in range(8)])  28.8 us
    ppermute x4, waiting for transfers between devices, with_halo(): after = lax.ppermute(leading, axis, down)  21.7 us
    ppermute x4, starting transfers between devices, with_halo(): after = lax.ppermute(leading, axis, down)  13.5 us
    ppermute x4, waiting for transfers between devices, with_halo(): before = lax.ppermute(last, axis, up)  6.89 us
    ppermute x4, starting transfers between devices, with_halo(): before = lax.ppermute(last, axis, up)  5.41 us
    ppermute x3, starting transfers between devices, shards(): lax.ppermute(totals, 'lon', [(dev, dev ^ hop) for dev in range(8)])  2.81 us
  transfers between devices with their start and end apart: 11, of which 9 were waited for; matrix products, arithmetic and copies ran while one was open for 1% of the time, Pallas kernels for 0%

profile of v1, /device:TPU:0, one launch (start us, length us, event | category | flops | bytes accessed | tf_op | source)
XLA Modules:
  0.0 89.4 jit_solution(8609111933586692719)
XLA Ops:
  0.0 0.8 convert_bitcast_fusion
  0.9 1.1 %pad_maximum_fusion.13 = f32[6,8,16,128]{3,2,1,0:T(8,128)S(1)} fusion(f32[1,8,16,128]{3,2,1,0:T(8,128)S(1)} %convert_bitcast_fusion, f32[1,8,16,128]{3,2,1,0:T(8,128)} %bitcast.19, f32[4,8,16,128]{3,2,1,0:T(8,128)} %param.5), kind=kLoop, calls=%fused_computation.18 | loop fusion | flops 196608 | bytes 786432 | tf_op jit(solution)/shard_map/concatenate | solution.py:87
  2.1 6.1 %collective-permute-start.1 = (f32[6,8,16,1]{3,2,1,0:T(8,128)S(1)}, f32[6,8,16,1]{3,2,1,0:T(8,128)S(1)}, u32[]{:S(2)}, u32[]{:S(2)}) collective-permute-start(f32[6,8,16,1]{3,2,1,0:T(8,128)S(1)} %get-tuple-element.24), channel_id=1, source_target_pairs={{4,0},{8,4},{12,8},{16,12},{20,16},{24,20},{28,24},{0,28},{5,1},{9... | collective-permute-start | bytes 9224 | tf_op jit(solution)/shard_map/ppermute | solution.py:23
  8.3 14.3 %collective-permute-done.1 = f32[6,8,16,1]{3,2,1,0:T(8,128)S(1)} collective-permute-done((f32[6,8,16,1]{3,2,1,0:T(8,128)S(1)}, f32[6,8,16,1]{3,2,1,0:T(8,128)S(1)}, u32[]{:S(2)}, u32[]{:S(2)}) %collective-permute-start.1) | collective-permute-done | bytes 3104 | tf_op jit(solution)/shard_map/ppermute | solution.py:23
  22.8 0.4 pad_maximum_fusion.15
  23.2 1.9 %collective-permute-start.2 = (f32[6,8,1,130]{3,2,1,0:T(1,128)S(1)}, f32[6,8,1,130]{3,2,1,0:T(1,128)S(1)}, u32[]{:S(2)}, u32[]{:S(2)}) collective-permute-start(f32[6,8,1,130]{3,2,1,0:T(1,128)S(1)} %get-tuple-element.10), channel_id=1, source_target_pairs={{0,1},{1,2},{2,3},{4,5},{5,6},{6,7},{8,9},{9,10},{10,11},{12,13},{... | collective-permute-start | bytes 74888 | tf_op jit(solution)/shard_map/ppermute | solution.py:22
  25.1 1.3 %collective-permute-start.3 = (f32[6,8,1,130]{3,2,1,0:T(1,128)S(1)}, f32[6,8,1,130]{3,2,1,0:T(1,128)S(1)}, u32[]{:S(2)}, u32[]{:S(2)}) collective-permute-start(f32[6,8,1,130]{3,2,1,0:T(1,128)S(1)} %get-tuple-element.9), channel_id=1, source_target_pairs={{1,0},{2,1},{3,2},{5,4},{6,5},{7,6},{9,8},{10,9},{11,10},{13,12},{... | collective-permute-start | bytes 74888 | tf_op jit(solution)/shard_map/ppermute | solution.py:23
  26.5 2.9 %collective-permute-done.3 = f32[6,8,1,130]{3,2,1,0:T(1,128)S(1)} collective-permute-done((f32[6,8,1,130]{3,2,1,0:T(1,128)S(1)}, f32[6,8,1,130]{3,2,1,0:T(1,128)S(1)}, u32[]{:S(2)}, u32[]{:S(2)}) %collective-permute-start.3) | collective-permute-done | bytes 24992 | tf_op jit(solution)/shard_map/ppermute | solution.py:23
  29.4 0.5 pad_maximum_fusion
  30.2 0.6 subtract_multiply_fusion.2
  31.2 0.3 subtract_multiply_fusion.3
  31.8 0.3 fusion.11
  32.2 4.8 %collective-permute-start.5 = (f32[4,8,16,1]{3,2,1,0:T(8,128)S(1)}, f32[4,8,16,1]{3,2,1,0:T(8,128)S(1)}, u32[]{:S(2)}, u32[]{:S(2)}) collective-permute-start(f32[4,8,16,1]{3,2,1,0:T(8,128)S(1)} %get-tuple-element.26), channel_id=1, source_target_pairs={{4,0},{8,4},{12,8},{16,12},{20,16},{24,20},{28,24},{0,28},{5,1},{9... | collective-permute-start | bytes 6152 | tf_op jit(solution)/shard_map/ppermute | solution.py:23
  37.0 0.3 fusion.36
  37.4 4.5 %collective-permute-done.5 = f32[4,8,16,1]{3,2,1,0:T(8,128)S(1)} collective-permute-done((f32[4,8,16,1]{3,2,1,0:T(8,128)S(1)}, f32[4,8,16,1]{3,2,1,0:T(8,128)S(1)}, u32[]{:S(2)}, u32[]{:S(2)}) %collective-permute-start.5) | collective-permute-done | bytes 2080 | tf_op jit(solution)/shard_map/ppermute | solution.py:23
  41.9 5.9 %collective-permute-done.4 = f32[4,8,16,1]{3,2,1,0:T(8,128)S(1)} collective-permute-done((f32[4,8,16,1]{3,2,1,0:T(8,128)S(1)}, f32[4,8,16,1]{3,2,1,0:T(8,128)S(1)}, u32[]{:S(2)}, u32[]{:S(2)}) %collective-permute-start.4) | collective-permute-done | bytes 2080 | tf_op jit(solution)/shard_map/ppermute | solution.py:22
  47.8 0.3 pad_maximum_fusion.22
  48.1 1.3 %collective-permute-start.7 = (f32[4,8,1,130]{3,2,1,0:T(1,128)S(1)}, f32[4,8,1,130]{3,2,1,0:T(1,128)S(1)}, u32[]{:S(2)}, u32[]{:S(2)}) collective-permute-start(f32[4,8,1,130]{3,2,1,0:T(1,128)S(1)} %get-tuple-element.18), channel_id=1, source_target_pairs={{1,0},{2,1},{3,2},{5,4},{6,5},{7,6},{9,8},{10,9},{11,10},{13,12},{... | collective-permute-start | bytes 49928 | tf_op jit(solution)/shard_map/ppermute | solution.py:23
  49.4 3.5 %collective-permute-start.6 = (f32[4,8,1,130]{3,2,1,0:T(1,128)S(1)}, f32[4,8,1,130]{3,2,1,0:T(1,128)S(1)}, u32[]{:S(2)}, u32[]{:S(2)}) collective-permute-start(f32[4,8,1,130]{3,2,1,0:T(1,128)S(1)} %get-tuple-element.17), channel_id=1, source_target_pairs={{0,1},{1,2},{2,3},{4,5},{5,6},{6,7},{8,9},{9,10},{10,11},{12,13},{... | collective-permute-start | bytes 49928 | tf_op jit(solution)/shard_map/ppermute | solution.py:22
  52.9 0.8 collective-permute-done.6
  53.7 0.4 pad_maximum_fusion.11
  54.1 0.6 subtract_multiply_fusion
  55.0 0.3 subtract_multiply_fusion.1
  55.4 0.3 fusion.4
  55.7 0.4 fusion.37
  56.2 2.1 %collective-permute-start.8 = (f32[512,128]{1,0:T(8,128)S(1)}, f32[512,128]{1,0:T(8,128)S(1)}, u32[]{:S(2)}, u32[]{:S(2)}) collective-permute-start(f32[512,128]{1,0:T(8,128)S(1)} %fusion.37), channel_id=1, source_target_pairs={{0,4},{4,0},{8,12},{12,8},{16,20},{20,16},{24,28},{28,24},{1,5},{5... | collective-permute-start | bytes 786440 | tf_op jit(solution)/shard_map/ppermute | solution.py:110
  58.3 6.3 %collective-permute-done.8 = f32[512,128]{1,0:T(8,128)S(1)} collective-permute-done((f32[512,128]{1,0:T(8,128)S(1)}, f32[512,128]{1,0:T(8,128)S(1)}, u32[]{:S(2)}, u32[]{:S(2)}) %collective-permute-start.8) | collective-permute-done | bytes 262176 | tf_op jit(solution)/shard_map/ppermute | solution.py:110
  64.8 8.8 %collective-permute-done.9 = f32[512,128]{1,0:T(8,128)S(1)} collective-permute-done((f32[512,128]{1,0:T(8,128)S(1)}, f32[512,128]{1,0:T(8,128)S(1)}, u32[]{:S(2)}, u32[]{:S(2)}) %collective-permute-start.9) | collective-permute-done | bytes 262176 | tf_op jit(solution)/shard_map/ppermute | solution.py:110
  73.6 0.6 collective-permute-start.10
  74.5 13.7 %collective-permute-done.10 = f32[512,128]{1,0:T(8,128)S(1)} collective-permute-done((f32[512,128]{1,0:T(8,128)S(1)}, f32[512,128]{1,0:T(8,128)S(1)}, u32[]{:S(2)}, u32[]{:S(2)}) %collective-permute-start.10) | collective-permute-done | bytes 262176 | tf_op jit(solution)/shard_map/ppermute | solution.py:110
  88.2 0.5 fusion.14
  88.7 0.7 multiply_add_fusion
  (48 shorter events, 2.5 us)
Async XLA Ops:
  0.8 22.0 %copy-start = (f32[4,8,16,128]{3,2,1,0:T(8,128)S(1)}, f32[4,8,16,128]{3,2,1,0:T(8,128)}, u32[]{:S(2)}) copy-start(f32[4,8,16,128]{3,2,1,0:T(8,128)} %param.5) | copy-start | bytes 786436
  0.8 22.0 %copy-start.1 = (f32[8,16,128]{2,1,0:T(8,128)S(1)}, f32[8,16,128]{2,1,0:T(8,128)}, u32[]{:S(2)}) copy-start(f32[8,16,128]{2,1,0:T(8,128)} %param.6) | copy-start | bytes 196612
  2.1 20.6 %collective-permute-start.1 = (f32[6,8,16,1]{3,2,1,0:T(8,128)S(1)}, f32[6,8,16,1]{3,2,1,0:T(8,128)S(1)}, u32[]{:S(2)}, u32[]{:S(2)}) collective-permute-start(f32[6,8,16,1]{3,2,1,0:T(8,128)S(1)} %get-tuple-element.24), channel_id=1, source_target_pairs={{4,0},{8,4},{12,8},{16,12},{20,16},{24,20},{28,24},{0,28},{5,1},{9... | collective-permute-start | bytes 9224 | tf_op jit(solution)/shard_map/ppermute | solution.py:23
  8.2 14.7 %collective-permute-start = (f32[6,8,16,1]{3,2,1,0:T(8,128)S(1)}, f32[6,8,16,1]{3,2,1,0:T(8,128)S(1)}, u32[]{:S(2)}, u32[]{:S(2)}) collective-permute-start(f32[6,8,16,1]{3,2,1,0:T(8,128)S(1)} %get-tuple-element.23), channel_id=1, source_target_pairs={{0,4},{4,8},{8,12},{12,16},{16,20},{20,24},{24,28},{28,0},{1,5},{5... | collective-permute-start | bytes 9224 | tf_op jit(solution)/shard_map/ppermute | solution.py:22
  23.2 3.3 %collective-permute-start.2 = (f32[6,8,1,130]{3,2,1,0:T(1,128)S(1)}, f32[6,8,1,130]{3,2,1,0:T(1,128)S(1)}, u32[]{:S(2)}, u32[]{:S(2)}) collective-permute-start(f32[6,8,1,130]{3,2,1,0:T(1,128)S(1)} %get-tuple-element.10), channel_id=1, source_target_pairs={{0,1},{1,2},{2,3},{4,5},{5,6},{6,7},{8,9},{9,10},{10,11},{12,13},{... | collective-permute-start | bytes 74888 | tf_op jit(solution)/shard_map/ppermute | solution.py:22
  25.1 4.3 %collective-permute-start.3 = (f32[6,8,1,130]{3,2,1,0:T(1,128)S(1)}, f32[6,8,1,130]{3,2,1,0:T(1,128)S(1)}, u32[]{:S(2)}, u32[]{:S(2)}) collective-permute-start(f32[6,8,1,130]{3,2,1,0:T(1,128)S(1)} %get-tuple-element.9), channel_id=1, source_target_pairs={{1,0},{2,1},{3,2},{5,4},{6,5},{7,6},{9,8},{10,9},{11,10},{13,12},{... | collective-permute-start | bytes 74888 | tf_op jit(solution)/shard_map/ppermute | solution.py:23
  32.2 9.6 %collective-permute-start.5 = (f32[4,8,16,1]{3,2,1,0:T(8,128)S(1)}, f32[4,8,16,1]{3,2,1,0:T(8,128)S(1)}, u32[]{:S(2)}, u32[]{:S(2)}) collective-permute-start(f32[4,8,16,1]{3,2,1,0:T(8,128)S(1)} %get-tuple-element.26), channel_id=1, source_target_pairs={{4,0},{8,4},{12,8},{16,12},{20,16},{24,20},{28,24},{0,28},{5,1},{9... | collective-permute-start | bytes 6152 | tf_op jit(solution)/shard_map/ppermute | solution.py:23
  37.0 10.8 %collective-permute-start.4 = (f32[4,8,16,1]{3,2,1,0:T(8,128)S(1)}, f32[4,8,16,1]{3,2,1,0:T(8,128)S(1)}, u32[]{:S(2)}, u32[]{:S(2)}) collective-permute-start(f32[4,8,16,1]{3,2,1,0:T(8,128)S(1)} %get-tuple-element.25), channel_id=1, source_target_pairs={{0,4},{4,8},{8,12},{12,16},{16,20},{20,24},{24,28},{28,0},{1,5},{5... | collective-permute-start | bytes 6152 | tf_op jit(solution)/shard_map/ppermute | solution.py:22
  48.1 4.8 %collective-permute-start.7 = (f32[4,8,1,130]{3,2,1,0:T(1,128)S(1)}, f32[4,8,1,130]{3,2,1,0:T(1,128)S(1)}, u32[]{:S(2)}, u32[]{:S(2)}) collective-permute-start(f32[4,8,1,130]{3,2,1,0:T(1,128)S(1)} %get-tuple-element.18), channel_id=1, source_target_pairs={{1,0},{2,1},{3,2},{5,4},{6,5},{7,6},{9,8},{10,9},{11,10},{13,12},{... | collective-permute-start | bytes 49928 | tf_op jit(solution)/shard_map/ppermute | solution.py:23
  49.4 4.3 %collective-permute-start.6 = (f32[4,8,1,130]{3,2,1,0:T(1,128)S(1)}, f32[4,8,1,130]{3,2,1,0:T(1,128)S(1)}, u32[]{:S(2)}, u32[]{:S(2)}) collective-permute-start(f32[4,8,1,130]{3,2,1,0:T(1,128)S(1)} %get-tuple-element.17), channel_id=1, source_target_pairs={{0,1},{1,2},{2,3},{4,5},{5,6},{6,7},{8,9},{9,10},{10,11},{12,13},{... | collective-permute-start | bytes 49928 | tf_op jit(solution)/shard_map/ppermute | solution.py:22
  55.7 9.0 %copy-start.3 = (s32[16]{0:T(128)S(1)}, s32[16]{0:T(128)}, u32[]{:S(2)}) copy-start(s32[16]{0:T(128)} %param.9) | copy-start | bytes 196
  55.7 9.0 %copy-start.2 = (s32[8,16,128]{2,1,0:T(8,128)S(1)}, s32[8,16,128]{2,1,0:T(8,128)}, u32[]{:S(2)}) copy-start(s32[8,16,128]{2,1,0:T(8,128)} %param.7) | copy-start | bytes 196612
  55.7 18.5 %copy-start.4 = (s32[16]{0:T(128)S(1)}, s32[16]{0:T(128)}, u32[]{:S(2)}) copy-start(s32[16]{0:T(128)} %param.8) | copy-start | bytes 196
  56.2 8.4 %collective-permute-start.8 = (f32[512,128]{1,0:T(8,128)S(1)}, f32[512,128]{1,0:T(8,128)S(1)}, u32[]{:S(2)}, u32[]{:S(2)}) collective-permute-start(f32[512,128]{1,0:T(8,128)S(1)} %fusion.37), channel_id=1, source_target_pairs={{0,4},{4,0},{8,12},{12,8},{16,20},{20,16},{24,28},{28,24},{1,5},{5... | collective-permute-start | bytes 786440 | tf_op jit(solution)/shard_map/ppermute | solution.py:110
  64.6 9.0 %collective-permute-start.9 = (f32[512,128]{1,0:T(8,128)S(1)}, f32[512,128]{1,0:T(8,128)S(1)}, u32[]{:S(2)}, u32[]{:S(2)}) collective-permute-start(f32[512,128]{1,0:T(8,128)S(1)} %add.125), channel_id=1, source_target_pairs={{0,8},{4,12},{8,0},{12,4},{16,24},{20,28},{24,16},{28,20},{1,9},{5... | collective-permute-start | bytes 786440 | tf_op jit(solution)/shard_map/ppermute | solution.py:110
  73.6 14.6 %collective-permute-start.10 = (f32[512,128]{1,0:T(8,128)S(1)}, f32[512,128]{1,0:T(8,128)S(1)}, u32[]{:S(2)}, u32[]{:S(2)}) collective-permute-start(f32[512,128]{1,0:T(8,128)S(1)} %add.126), channel_id=1, source_target_pairs={{0,16},{4,20},{8,24},{12,28},{16,0},{20,4},{24,8},{28,12},{1,17},{... | collective-permute-start | bytes 786440 | tf_op jit(solution)/shard_map/ppermute | solution.py:110
